TPU v7x, 256 devices: a whole 4x4x8 slice. The times are simulated.
256 devices in a mesh: order: 64 (over z, x, core), lat: 4 (over y).
Axes of the slice: x: 4, y: 4, z: 8, core: 2. Of those that a mesh axis runs over, the one named last changes fastest.
Arguments:
- position: float32 [128, 2, 64, 2160], P('order', None, None, 'lat'), may hold values from -6 to 6
- residual: float32 [128, 2, 64, 2160], P('order', None, None, 'lat'), as said below
- direction: float32 [128, 2, 64, 2160], P('order', None, None, 'lat'), as said below
- legendre: float32 [128, 2160, 2048], P('order', None, 'lat'), may hold values from -0.125 to 0.125
- order_of: int32 [128], replicated, may hold values from 0 to 2032, as said below
- class_idx: int32 [2048, 4320], P(('lat', 'order')), may hold values from 0 to 15
- land: int32 [2048, 4320], P(('lat', 'order')), may hold values 0 or 1
- class_weight: float32 [16, 2], replicated, may hold values from 0.2 to 5
- damping: float32 [2160], P('lat'), may hold values from 0.05 to 0.5
Outputs:
- new_position: float32 [128, 2, 64, 2160], P('order', None, None, 'lat')
- new_residual: float32 [128, 2, 64, 2160], P('order', None, None, 'lat')
- new_direction: float32 [128, 2, 64, 2160], P('order', None, None, 'lat')
Inputs may be any that keep to these rules, and one draw needn't show every extreme that they name: `order_of`: distinct multiples of 16: each of 0, 16, ..., 16 * (128 - 1) appears exactly once. `residual`: real-valued and not zero. `direction`: real-valued and not zero.
All inputs are finite; a program needn't handle non-finite values. No bound on the sum of `land` on one device may be relied on, other than what follows from the above.
Results may differ from a plain program's by a relative error of at most 0.000058.
Values sent between devices are 32-bit elements; how exact they have to be, the bound alone decides.
A program may use at most 128 MiB of HBM per device.

v0:
```python
import math
import jax
import jax.numpy as jnp
from jax import lax
from jax.sharding import PartitionSpec as P


def tables(order_of, longitudes):
    longitude = jnp.arange(longitudes, dtype=jnp.int32)
    phases = order_of[:, None] * longitude[None, :] % longitudes
    angles = phases.astype(jnp.float32) * (2.0 * math.pi / longitudes)
    return jnp.stack([jnp.cos(angles), jnp.sin(angles)])


def sample_sums(product):
    return jnp.sum(product, axis=(0, 1, 3))


def shards(
    position, residual, direction, legendre, order_of, class_idx, land, class_weight, damping
):
    highest = lax.Precision.HIGHEST
    m_local = position.shape[0]
    samples = position.shape[2]
    deg_local = position.shape[3]
    band_rows = legendre.shape[2]
    lat_index = lax.axis_index("lat")
    order_index = lax.axis_index("order")
    my_orders = lax.dynamic_slice_in_dim(order_of, order_index * m_local, m_local)
    deg_start = lat_index * deg_local
    own_degrees = deg_start + jnp.arange(deg_local, dtype=jnp.int32)
    own_valid = (own_degrees[None, :] >= my_orders[:, None]).astype(jnp.float32)[:, None, None, :]
    pos_m = position * own_valid
    res_m = residual * own_valid
    dir_m = direction * own_valid
    norm_before = lax.psum(sample_sums(res_m * res_m), ("order", "lat"))
    block_part = lax.all_gather(direction, "lat", axis=3, tiled=True)
    degree_count = block_part.shape[3]
    in_block = jnp.arange(degree_count, dtype=jnp.int32)
    in_triangle = (in_block[None, :] >= my_orders[:, None]).astype(jnp.float32)
    masked = block_part * in_triangle[:, None, None, :]
    synthesis = jnp.einsum("mskd,mdt->mtsk", masked, legendre, precision=highest)
    grid_in = lax.all_to_all(
        synthesis.reshape(m_local, band_rows, 2 * samples),
        "order",
        split_axis=1,
        concat_axis=0,
        tiled=True,
    )
    orders_all = grid_in.shape[0]
    rows_here = grid_in.shape[1]
    grid_in = grid_in.reshape(orders_all, rows_here, 2, samples)
    longitudes = class_idx.shape[1]
    harmonic = tables(order_of, longitudes)
    surface = jnp.einsum("mrsk,sml->rkl", grid_in, harmonic, precision=highest)
    class_count = class_weight.shape[0]
    onehot = (
        class_idx[:, :, None] == jnp.arange(class_count, dtype=jnp.int32)[None, None, :]
    ).astype(jnp.float32)
    by_class = jnp.dot(onehot, class_weight, precision=highest)
    weight_grid = jnp.where(land == 1, by_class[:, :, 1], by_class[:, :, 0])
    weighted = surface * weight_grid[:, None, :]
    spectra = jnp.einsum("rkl,sml->mrsk", weighted, harmonic, precision=highest) * (
        2.0 / longitudes
    )
    returned = lax.all_to_all(
        spectra.reshape(orders_all, rows_here, 2 * samples),
        "order",
        split_axis=0,
        concat_axis=1,
        tiled=True,
    )
    returned = returned.reshape(m_local, band_rows, 2, samples)
    band_part = jnp.einsum("mtsk,mdt->mskd", returned, legendre, precision=highest)
    totals = lax.psum(band_part, "lat")
    summed = lax.dynamic_slice_in_dim(totals, deg_start, deg_local, 3)
    applied = (summed + damping[None, None, None, :] * dir_m) * own_valid
    curvature_sum = lax.psum(sample_sums(dir_m * applied), ("order", "lat"))
    step_size = (norm_before / curvature_sum)[None, None, :, None]
    new_residual = res_m - step_size * applied
    norm_after = lax.psum(sample_sums(new_residual * new_residual), ("order", "lat"))
    ratio_new = (norm_after / norm_before)[None, None, :, None]
    new_position = pos_m + step_size * dir_m
    new_direction = new_residual + ratio_new * dir_m
    return (new_position, new_residual, new_direction)


def solution(mesh):
    return jax.shard_map(
        shards,
        mesh=mesh,
        in_specs=(
            P("order", None, None, "lat"),
            P("order", None, None, "lat"),
            P("order", None, None, "lat"),
            P("order", None, "lat"),
            P(),
            P(("lat", "order"), None),
            P(("lat", "order"), None),
            P(),
            P("lat"),
        ),
        out_specs=(
            P("order", None, None, "lat"),
            P("order", None, None, "lat"),
            P("order", None, None, "lat"),
        ),
        check_vma=False,
    )
```

profile of v0, /device:TPU:1, one launch (start us, length us, event | category | flops | bytes accessed | tf_op | source)
XLA Modules:
  0.0 419.9 jit_solution(14200132624685688203)
XLA Ops:
  7.2 0.0 copy-start
  7.2 0.0 all-gather.2.cloned.1.call-start
  7.2 2.3 copy.20
  9.6 0.0 all-gather.2.cloned.1.call-update
  9.6 0.1 dynamic_slice.6
  9.7 0.7 fusion.11
  10.4 0.1 fusion.30
  10.6 0.9 fusion.37
  11.4 9.9 %fusion.17 = (f32[1,128,4320]{1,2,0:T(8,128)S(1)}, f32[1,128,4320]{1,2,0:T(8,128)}) fusion(s32[128]{0:T(128)S(1)} %copy-done.10), kind=kLoop, calls=%fused_computation.23 | loop fusion | flops 4976640 | bytes 4424192 | tf_op jit(solution)/shard_map/cos | solution.py:12
  21.3 44.9 %all-gather.2.cloned.1.call-done = f32[2,2,64,2160]{2,1,0,3:T(2,128)} async-done(((f32[2,2,64,540]{2,1,0,3:T(2,128)}), f32[2,2,64,2160]{2,1,0,3:T(2,128)}) %all-gather.2.cloned.1.call-update) | async-done | bytes 2211856 | tf_op jit(solution)/shard_map/all_gather | solution.py:37
  66.2 6.6 %broadcast_multiply_fusion = f32[2,2,64,2160]{2,1,0,3:T(2,128)S(1)} fusion(f32[2,2,64,2160]{2,1,0,3:T(2,128)} %all-gather.2.cloned.1.call-done, f32[2,2160]{0,1:T(8,128)S(1)} %fusion.30), kind=kLoop, calls=%fused_computation.18 | loop fusion | flops 552960 | bytes 4440960 | tf_op jit(solution)/shard_map/mul | solution.py:41
  72.8 8.7 %fusion.4 = f32[2,2,64,512]{3,2,1,0:T(8,128)S(1)} fusion(f32[2,2160,512]{2,1,0:T(8,128)S(1)} %copy-done.1, f32[2,2,64,2160]{2,1,0,3:T(2,128)S(1)} %broadcast_multiply_fusion), kind=kOutput, calls=%fused_computation.5 | convolution fusion | flops 3397386240 | bytes 11583488 | tf_op jit(solution)/shard_map/mskd,mdt->mtsk/dot_general | solution.py:42
  81.5 1.0 copy.22
  82.5 10.8 %all-to-all-start = ((f32[2,512,128]{2,0,1:T(2,128)}), f32[2,512,128]{2,0,1:T(2,128)S(1)}, u32[]{:S(2)}, u32[]{:S(2)}) async-start(f32[2,512,128]{2,0,1:T(2,128)} %copy.22), calls=%async_computation | async-start | bytes 1048576 | tf_op jit(solution)/shard_map/all_to_all | solution.py:43
  93.3 0.2 all-reduce.3.cloned.1.call-start
  93.6 17.4 %all-to-all-done = f32[2,512,128]{2,0,1:T(2,128)S(1)} async-done(((f32[2,512,128]{2,0,1:T(2,128)}), f32[2,512,128]{2,0,1:T(2,128)S(1)}, u32[]{:S(2)}, u32[]{:S(2)}) %all-to-all-start) | async-done | bytes 524320 | tf_op jit(solution)/shard_map/all_to_all | solution.py:43
  111.0 0.8 copy.24
  111.9 1.6 reshape.148
  113.5 31.3 %fusion.8 = f32[8,64,4320,1]{2,1,3,0:T(8,128)S(1)} fusion(f32[1,128,4320]{1,2,0:T(8,128)} %get-tuple-element.13, f32[1,128,4320]{1,2,0:T(8,128)S(1)} %get-tuple-element.12, f32[128,8,2,64]{3,2,1,0:T(2,128)S(1)} %reshape.148), kind=kOutput, calls=%fused_computation.10 | convolution fusion | flops 6795878400 | bytes 13795328 | tf_op jit(solution)/shard_map/mrsk,sml->rkl/dot_general | solution.py:55
  144.8 7.8 %fusion.24 = f32[128,8,2,64]{0,3,1,2:T(8,128)S(1)} fusion(f32[8,64,4320,1]{2,1,3,0:T(8,128)S(1)} %fusion.8, f32[8,4320]{1,0:T(8,128)S(1)} %fusion.33, f32[1,128,4320]{1,2,0:T(8,128)S(1)} %copy-done.2, f32[1,128,4320]{1,2,0:T(8,128)S(1)} %get-tuple-element.12), kind=kOutput, calls=%fused_computation.26 | convolution fusion | flops 6798221312 | bytes 13933568 | tf_op jit(solution)/shard_map/rkl,sml->mrsk/dot_general | solution.py:63
  152.7 0.2 copy.28
  153.0 23.3 %all_to_all.30 = f32[128,8,128]{2,1,0:T(8,128)S(1)} all-to-all(f32[128,8,128]{2,1,0:T(8,128)S(1)} %copy.28), channel_id=1, replica_groups=mesh['order'=64,'lat'=4] {'order'}, dimensions={0} | all-to-all | bytes 1048576 | tf_op jit(solution)/shard_map/all_to_all | solution.py:66
  176.3 0.6 reshape.150
  176.9 19.2 %fusion.2 = f32[2,2,64,2160]{3,2,1,0:T(8,128)} fusion(f32[2,2160,512]{2,1,0:T(8,128)} %param.12, f32[2,512,2,64]{3,2,1,0:T(2,128)S(1)} %reshape.150), kind=kOutput, calls=%fused_computation.3 | convolution fusion | flops 3397386240 | bytes 11583488 | tf_op jit(solution)/shard_map/mtsk,mdt->mskd/dot_general | solution.py:74
  196.2 0.0 all-reduce.3.cloned.1.call-update
  196.2 0.1 compare_convert_fusion
  196.3 61.3 %all-reduce.3.cloned.1.call-done = f32[2,2,64,2160]{3,2,1,0:T(8,128)} async-done(((f32[2,2,64,2160]{3,2,1,0:T(8,128)}), f32[2,2,64,2160]{3,2,1,0:T(8,128)}) %all-reduce.3.cloned.1.call-update) | async-done | bytes 2211856 | tf_op jit(solution)/shard_map/psum | solution.py:75
  257.6 1.6 multiply_reduce_fusion.1
  259.2 76.0 %all-reduce = (f32[64]{0:T(128)S(1)}, f32[64]{0:T(128)S(1)}) all-reduce(f32[64]{0:T(128)S(1)} %get-tuple-element.4, f32[64]{0:T(128)S(1)} %get-tuple-element.3), channel_id=1, replica_groups=mesh['order'=64,'lat'=4] {'order','lat'}, use_global_device_ids=true, to_apply=%region_1.0 | all-reduce | flops 128 | bytes 1024 | tf_op jit(solution)/shard_map/psum | solution.py:36
  335.1 2.5 multiply_reduce_fusion
  337.6 74.3 %psum.31 = f32[64]{0:T(128)S(1)} all-reduce(f32[64]{0:T(128)S(1)} %get-tuple-element.7), channel_id=1, replica_groups=mesh['order'=64,'lat'=4] {'order','lat'}, use_global_device_ids=true, to_apply=%region_6.7 | all-reduce | flops 64 | bytes 512 | tf_op jit(solution)/shard_map/psum | solution.py:81
  411.9 1.0 multiply_add_fusion
  (30 shorter events, 0.2 us)
Async XLA Ops:
  7.2 2.5 copy-start
  7.2 2.4 copy-start.10
  7.2 2.5 copy-start.11
  7.2 59.0 %all-gather.2.cloned.1.call-start = ((), (), s32[]{:S(2)}) async-start(), calls=%async_computation.2 | async-start | bytes 5529600 | tf_op jit(solution)/shard_map/all_gather | solution.py:37
  66.2 6.6 %copy-start.1 = (f32[2,2160,512]{2,1,0:T(8,128)S(1)}, f32[2,2160,512]{2,1,0:T(8,128)}, u32[]{:S(2)}) copy-start(f32[2,2160,512]{2,1,0:T(8,128)} %param.12) | copy-start | bytes 26542084
  72.7 20.8 %copy-start.7 = (f32[8,4320,1]{1,2,0:T(1,128)S(1)}, f32[8,4320,1]{1,2,0:T(1,128)}, u32[]{:S(2)}) copy-start(f32[8,4320,1]{1,2,0:T(1,128)} %get-tuple-element.11) | copy-start | bytes 414724
  72.8 20.8 %copy-start.8 = (s32[8,4320]{1,0:T(8,128)S(1)}, s32[8,4320]{1,0:T(8,128)}, u32[]{:S(2)}) copy-start(s32[8,4320]{1,0:T(8,128)} %param.15) | copy-start | bytes 414724
  82.5 28.5 %all-to-all-start = ((f32[2,512,128]{2,0,1:T(2,128)}), f32[2,512,128]{2,0,1:T(2,128)S(1)}, u32[]{:S(2)}, u32[]{:S(2)}) async-start(f32[2,512,128]{2,0,1:T(2,128)} %copy.22), calls=%async_computation | async-start | bytes 1048576 | tf_op jit(solution)/shard_map/all_to_all | solution.py:43
  93.3 164.3 %all-reduce.3.cloned.1.call-start = ((), (), s32[]{:S(2)}) async-start(), calls=%async_computation.3 | async-start | bytes 4456448 | tf_op jit(solution)/shard_map/psum | solution.py:75
  113.5 31.3 %copy-start.2 = (f32[1,128,4320]{1,2,0:T(8,128)S(1)}, f32[1,128,4320]{1,2,0:T(8,128)}, u32[]{:S(2)}) copy-start(f32[1,128,4320]{1,2,0:T(8,128)} %get-tuple-element.13) | copy-start | bytes 6635524
  196.2 61.4 %copy-start.3 = (f32[2,2,64,540]{3,2,1,0:T(8,128)S(1)}, f32[2,2,64,540]{3,2,1,0:T(8,128)}, u32[]{:S(2)}) copy-start(f32[2,2,64,540]{3,2,1,0:T(8,128)} %param.11) | copy-start | bytes 1658884
  196.2 61.4 %copy-start.4 = (f32[2,2,64,540]{3,2,1,0:T(8,128)S(1)}, f32[2,2,64,540]{3,2,1,0:T(8,128)}, u32[]{:S(2)}) copy-start(f32[2,2,64,540]{3,2,1,0:T(8,128)} %param.10) | copy-start | bytes 1658884
  196.2 61.4 %copy-start.9 = (f32[540]{0:T(1024)S(1)}, f32[540]{0:T(1024)}, u32[]{:S(2)}) copy-start(f32[540]{0:T(1024)} %param.17) | copy-start | bytes 6484
  196.2 138.9 %copy-start.6 = (f32[2,2,64,540]{3,2,1,0:T(8,128)S(1)}, f32[2,2,64,540]{3,2,1,0:T(8,128)}, u32[]{:S(2)}) copy-start(f32[2,2,64,540]{3,2,1,0:T(8,128)} %param.9) | copy-start | bytes 1658884
  337.6 75.3 %copy-start.5 = (f32[2,2,64,540]{3,2,1,0:T(8,128)}, f32[2,2,64,540]{3,2,1,0:T(8,128)S(1)}, u32[]{:S(2)}) copy-start(f32[2,2,64,540]{3,2,1,0:T(8,128)S(1)} %get-tuple-element.8) | copy-start | bytes 1658884
Sparse Core Ops, SparseCore 0:
  9.8 56.2 all-gather.1
  196.3 61.1 all-reduce.2
where the time goes:
time: 429 us; the launch traced here: 420 us
  blocking collectives  174 us (41%)
  waiting for transfers between devices  124 us (29%)
  matrix products  67.8 us (16%)
  other arithmetic  21.7 us (5%)
  between operations  14.5 us (3%)
  starting transfers between devices  11.1 us (3%)
  local copies, waits for them, and re-layouts  7.76 us (2%)
    psum x1, blocking collectives, shards(): norm_before = lax.psum(sample_sums(res_m * res_m), ('order', 'lat'))  76 us
    psum x1, blocking collectives, shards(): lax.psum(sample_sums(new_residual * new_residual), ('order', 'lat'))  74.3 us
    psum x1, waiting for transfers between devices, shards(): totals = lax.psum(band_part, 'lat')  61.3 us
    all_gather x1, waiting for transfers between devices, shards(): block_part = lax.all_gather(direction, 'lat', axis=3, tiled=True)  44.9 us
    dot_general x1, matrix products, shards(): surface = jnp.einsum('mrsk,sml->rkl', grid_in, harmonic, precision=highest)  31.3 us
    all_to_all x1, blocking collectives, shards(): lax.all_to_all(spectra.reshape(orders_all, rows_here, 2 * samples), 'orde...  23.3 us
    dot_general x1, matrix products, shards(): jnp.einsum('mtsk,mdt->mskd', returned, legendre, precision=highest)  19.2 us
    all_to_all x1, waiting for transfers between devices, shards(): lax.all_to_all(synthesis.reshape(m_local, band_rows, 2 * samples), 'order...  17.4 us
  transfers between devices with their start and end apart: 3, of which 3 were waited for; matrix products, arithmetic and copies ran while one was open for 3% of the time, Pallas kernels for 0%

commit v1 on v0

--- a/solution.py
+++ b/solution.py
@@ -34,7 +34,11 @@
     res_m = residual * own_valid
     dir_m = direction * own_valid
     norm_before = lax.psum(sample_sums(res_m * res_m), ("order", "lat"))
-    block_part = lax.all_gather(direction, "lat", axis=3, tiled=True)
+    series = []
+    for _ in range(jax.lax.axis_size("lat")):
+        series.append(direction)
+    opened = jax.lax.all_to_all(jnp.stack(series), "lat", 0, 0)
+    block_part = jnp.concatenate(opened, axis=3)
     degree_count = block_part.shape[3]
     in_block = jnp.arange(degree_count, dtype=jnp.int32)
     in_triangle = (in_block[None, :] >= my_orders[:, None]).astype(jnp.float32)

time: 429 us -> 412 us (0.960)
  waiting for transfers between devices: 124 us -> 96.8 us
  starting transfers between devices: 11.1 us -> 20.1 us
  local copies, waits for them, and re-layouts: 7.76 us -> 16.5 us
  other arithmetic: 21.7 us -> 15.1 us
    all_gather x1 -> x0, waiting for transfers between devices: 44.9 us -> none  [shards(): block_part = lax.all_gather(direction, 'lat', axis=3, tiled=True)]
    all_to_all x0 -> x1, waiting for transfers between devices: none -> 19 us  [shards(): opened = jax.lax.all_to_all(jnp.stack(series), 'lat', 0, 0)]
    reshape x0 -> x2, local copies, waits for them, and re-layouts: none -> 8.87 us  [shards(): block_part = jnp.concatenate(opened, axis=3)]
    mul x1 -> x0, other arithmetic: 6.57 us -> none  [shards(): masked = block_part * in_triangle[:, None, None, :]]
    all_to_all x0 -> x1, starting transfers between devices: none -> 5.13 us  [shards(): opened = jax.lax.all_to_all(jnp.stack(series), 'lat', 0, 0)]
where the time goes in v1:
time: 412 us; the launch traced here: 405 us
  blocking collectives  174 us (42%)
  waiting for transfers between devices  96.8 us (23%)
  matrix products  68 us (17%)
  starting transfers between devices  20.1 us (5%)
  local copies, waits for them, and re-layouts  16.5 us (4%)
  other arithmetic  15.1 us (4%)
  between operations  14.4 us (3%)
    psum x1, blocking collectives, shards(): norm_before = lax.psum(sample_sums(res_m * res_m), ('order', 'lat'))  76 us
    psum x1, blocking collectives, shards(): lax.psum(sample_sums(new_residual * new_residual), ('order', 'lat'))  74.3 us
    psum x1, waiting for transfers between devices, shards(): totals = lax.psum(band_part, 'lat')  60.3 us
    dot_general x1, matrix products, shards(): surface = jnp.einsum('mrsk,sml->rkl', grid_in, harmonic, precision=highest)  31.3 us
    all_to_all x1, blocking collectives, shards(): lax.all_to_all(spectra.reshape(orders_all, rows_here, 2 * samples), 'orde...  23.3 us
    dot_general x1, matrix products, shards(): jnp.einsum('mtsk,mdt->mskd', returned, legendre, precision=highest)  19.3 us
    all_to_all x1, waiting for transfers between devices, shards(): opened = jax.lax.all_to_all(jnp.stack(series), 'lat', 0, 0)  19 us
    all_to_all x1, waiting for transfers between devices, shards(): lax.all_to_all(synthesis.reshape(m_local, band_rows, 2 * samples), 'order...  17.4 us
  transfers between devices with their start and end apart: 3, of which 3 were waited for; matrix products, arithmetic and copies ran while one was open for 3% of the time, Pallas kernels for 0%

profile of v1, /device:TPU:1, one launch (start us, length us, event | category | flops | bytes accessed | tf_op | source)
XLA Modules:
  0.0 404.5 jit_solution(17633733282573837712)
XLA Ops:
  7.2 0.0 copy-start
  7.2 2.9 stack.5
  10.0 5.1 %all-to-all-start = ((f32[4,2,2,64,540]{4,3,2,1,0:T(8,128)}), f32[4,2,2,64,540]{4,3,2,1,0:T(8,128)}, u32[]{:S(2)}, u32[]{:S(2)}) async-start(f32[4,2,2,64,540]{4,3,2,1,0:T(8,128)} %stack.5), calls=%async_computation | async-start | bytes 5242880 | tf_op jit(solution)/shard_map/all_to_all | solution.py:40
  15.2 0.7 fusion.11
  15.9 0.2 fusion.37
  16.2 0.1 dynamic_slice.6
  16.2 0.1 compare_convert_fusion
  16.3 9.9 %fusion.17 = (f32[1,128,4320]{1,2,0:T(8,128)S(1)}, f32[1,128,4320]{1,2,0:T(8,128)}) fusion(s32[128]{0:T(128)S(1)} %copy-done.8), kind=kLoop, calls=%fused_computation.22 | loop fusion | flops 4976640 | bytes 4424192 | tf_op jit(solution)/shard_map/cos | solution.py:12
  26.2 19.0 %all-to-all-done = f32[4,2,2,64,540]{4,3,2,1,0:T(8,128)} async-done(((f32[4,2,2,64,540]{4,3,2,1,0:T(8,128)}), f32[4,2,2,64,540]{4,3,2,1,0:T(8,128)}, u32[]{:S(2)}, u32[]{:S(2)}) %all-to-all-start) | async-done | bytes 2211872 | tf_op jit(solution)/shard_map/all_to_all | solution.py:40
  45.2 4.9 %copy.29 = f32[2,2,64,4,540]{4,3,2,1,0:T(4,128)} copy(f32[2,2,64,4,540]{4,2,1,0,3:T(8,128)} %bitcast.2) | data formatting | bytes 4423680 | tf_op jit(solution)/shard_map/reshape | solution.py:41
  50.1 3.9 reshape.156
  54.1 8.9 %fusion.4 = f32[2,2,64,512]{3,2,1,0:T(8,128)S(1)} fusion(f32[2,2160,512]{2,1,0:T(8,128)} %param.12, f32[2,2,64,2160]{3,2,1,0:T(8,128)} %reshape.156, f32[2,2160]{1,0:T(2,128)S(1)} %compare_convert_fusion), kind=kOutput, calls=%fused_computation.5 | convolution fusion | flops 3397939200 | bytes 11600768 | tf_op jit(solution)/shard_map/mskd,mdt->mtsk/dot_general | solution.py:46
  63.0 1.0 copy.30
  64.0 14.8 %all-to-all-start.1 = ((f32[2,512,128]{2,0,1:T(2,128)}), f32[2,512,128]{2,0,1:T(2,128)S(1)}, u32[]{:S(2)}, u32[]{:S(2)}) async-start(f32[2,512,128]{2,0,1:T(2,128)} %copy.30), calls=%async_computation.1 | async-start | bytes 1048576 | tf_op jit(solution)/shard_map/all_to_all | solution.py:47
  78.8 0.2 all-reduce.3.cloned.1.call-start
  79.1 17.4 %all-to-all-done.1 = f32[2,512,128]{2,0,1:T(2,128)S(1)} async-done(((f32[2,512,128]{2,0,1:T(2,128)}), f32[2,512,128]{2,0,1:T(2,128)S(1)}, u32[]{:S(2)}, u32[]{:S(2)}) %all-to-all-start.1) | async-done | bytes 524320 | tf_op jit(solution)/shard_map/all_to_all | solution.py:47
  96.5 0.8 copy.32
  97.3 1.6 reshape.158
  99.0 31.3 %fusion.8 = f32[8,64,4320,1]{2,1,3,0:T(8,128)S(1)} fusion(f32[1,128,4320]{1,2,0:T(8,128)} %get-tuple-element.13, f32[1,128,4320]{1,2,0:T(8,128)S(1)} %get-tuple-element.12, f32[128,8,2,64]{3,2,1,0:T(2,128)S(1)} %reshape.158), kind=kOutput, calls=%fused_computation.10 | convolution fusion | flops 6795878400 | bytes 13795328 | tf_op jit(solution)/shard_map/mrsk,sml->rkl/dot_general | solution.py:59
  130.3 7.8 %fusion.24 = f32[128,8,2,64]{0,3,1,2:T(8,128)S(1)} fusion(f32[8,64,4320,1]{2,1,3,0:T(8,128)S(1)} %fusion.8, f32[8,4320]{1,0:T(8,128)S(1)} %fusion.33, f32[1,128,4320]{1,2,0:T(8,128)S(1)} %copy-done.1, f32[1,128,4320]{1,2,0:T(8,128)S(1)} %get-tuple-element.12), kind=kOutput, calls=%fused_computation.25 | convolution fusion | flops 6798221312 | bytes 13933568 | tf_op jit(solution)/shard_map/rkl,sml->mrsk/dot_general | solution.py:67
  138.2 0.2 copy.36
  138.4 23.3 %all_to_all.35 = f32[128,8,128]{2,1,0:T(8,128)S(1)} all-to-all(f32[128,8,128]{2,1,0:T(8,128)S(1)} %copy.36), channel_id=1, replica_groups=mesh['order'=64,'lat'=4] {'order'}, dimensions={0} | all-to-all | bytes 1048576 | tf_op jit(solution)/shard_map/all_to_all | solution.py:70
  161.8 0.6 reshape.160
  162.4 19.3 %fusion.2 = f32[2,2,64,2160]{3,2,1,0:T(8,128)} fusion(f32[2,2160,512]{2,1,0:T(8,128)} %param.12, f32[2,512,2,64]{3,2,1,0:T(2,128)S(1)} %reshape.160), kind=kOutput, calls=%fused_computation.3 | convolution fusion | flops 3397386240 | bytes 11583488 | tf_op jit(solution)/shard_map/mtsk,mdt->mskd/dot_general | solution.py:78
  181.7 0.0 all-reduce.3.cloned.1.call-update
  181.7 0.1 compare_convert_fusion.1
  181.8 60.3 %all-reduce.3.cloned.1.call-done = f32[2,2,64,2160]{3,2,1,0:T(8,128)} async-done(((f32[2,2,64,2160]{3,2,1,0:T(8,128)}), f32[2,2,64,2160]{3,2,1,0:T(8,128)}) %all-reduce.3.cloned.1.call-update) | async-done | bytes 2211856 | tf_op jit(solution)/shard_map/psum | solution.py:79
  242.2 1.6 multiply_reduce_fusion.1
  243.7 76.0 %all-reduce = (f32[64]{0:T(128)S(1)}, f32[64]{0:T(128)S(1)}) all-reduce(f32[64]{0:T(128)S(1)} %get-tuple-element.4, f32[64]{0:T(128)S(1)} %get-tuple-element.3), channel_id=1, replica_groups=mesh['order'=64,'lat'=4] {'order','lat'}, use_global_device_ids=true, to_apply=%region_1.0 | all-reduce | flops 128 | bytes 1024 | tf_op jit(solution)/shard_map/psum | solution.py:36
  319.7 2.5 multiply_reduce_fusion
  322.2 74.3 %psum.31 = f32[64]{0:T(128)S(1)} all-reduce(f32[64]{0:T(128)S(1)} %get-tuple-element.7), channel_id=1, replica_groups=mesh['order'=64,'lat'=4] {'order','lat'}, use_global_device_ids=true, to_apply=%region_6.7 | all-reduce | flops 64 | bytes 512 | tf_op jit(solution)/shard_map/psum | solution.py:85
  396.5 1.0 multiply_add_fusion
  (26 shorter events, 0.2 us)
Async XLA Ops:
  7.2 8.0 %copy-start = (f32[16,2]{0,1:T(2,128)S(1)}, f32[16,2]{0,1:T(2,128)}, u32[]{:S(2)}) copy-start(f32[16,2]{0,1:T(2,128)} %param.16) | copy-start | bytes 388
  10.0 5.1 %copy-start.9 = (s32[8,4320]{1,0:T(8,128)S(1)}, s32[8,4320]{1,0:T(8,128)}, u32[]{:S(2)}) copy-start(s32[8,4320]{1,0:T(8,128)} %param.14) | copy-start | bytes 414724
  10.0 6.1 %copy-start.8 = (s32[128]{0:T(128)S(1)}, s32[128]{0:T(128)}, u32[]{:S(2)}) copy-start(s32[128]{0:T(128)} %param.13) | copy-start | bytes 1540
  10.0 35.2 %all-to-all-start = ((f32[4,2,2,64,540]{4,3,2,1,0:T(8,128)}), f32[4,2,2,64,540]{4,3,2,1,0:T(8,128)}, u32[]{:S(2)}, u32[]{:S(2)}) async-start(f32[4,2,2,64,540]{4,3,2,1,0:T(8,128)} %stack.5), calls=%async_computation | async-start | bytes 5242880 | tf_op jit(solution)/shard_map/all_to_all | solution.py:40
  54.1 24.9 %copy-start.6 = (s32[8,4320]{1,0:T(8,128)S(1)}, s32[8,4320]{1,0:T(8,128)}, u32[]{:S(2)}) copy-start(s32[8,4320]{1,0:T(8,128)} %param.15) | copy-start | bytes 414724
  64.0 32.5 %all-to-all-start.1 = ((f32[2,512,128]{2,0,1:T(2,128)}), f32[2,512,128]{2,0,1:T(2,128)S(1)}, u32[]{:S(2)}, u32[]{:S(2)}) async-start(f32[2,512,128]{2,0,1:T(2,128)} %copy.30), calls=%async_computation.1 | async-start | bytes 1048576 | tf_op jit(solution)/shard_map/all_to_all | solution.py:47
  78.8 163.4 %all-reduce.3.cloned.1.call-start = ((), (), s32[]{:S(2)}) async-start(), calls=%async_computation.3 | async-start | bytes 4456448 | tf_op jit(solution)/shard_map/psum | solution.py:79
  99.0 31.3 %copy-start.1 = (f32[1,128,4320]{1,2,0:T(8,128)S(1)}, f32[1,128,4320]{1,2,0:T(8,128)}, u32[]{:S(2)}) copy-start(f32[1,128,4320]{1,2,0:T(8,128)} %get-tuple-element.13) | copy-start | bytes 6635524
  181.7 60.5 %copy-start.2 = (f32[2,2,64,540]{3,2,1,0:T(8,128)S(1)}, f32[2,2,64,540]{3,2,1,0:T(8,128)}, u32[]{:S(2)}) copy-start(f32[2,2,64,540]{3,2,1,0:T(8,128)} %param.11) | copy-start | bytes 1658884
  181.7 60.5 %copy-start.3 = (f32[2,2,64,540]{3,2,1,0:T(8,128)S(1)}, f32[2,2,64,540]{3,2,1,0:T(8,128)}, u32[]{:S(2)}) copy-start(f32[2,2,64,540]{3,2,1,0:T(8,128)} %param.10) | copy-start | bytes 1658884
  181.7 60.5 %copy-start.7 = (f32[540]{0:T(1024)S(1)}, f32[540]{0:T(1024)}, u32[]{:S(2)}) copy-start(f32[540]{0:T(1024)} %param.17) | copy-start | bytes 6484
  181.7 138.0 %copy-start.5 = (f32[2,2,64,540]{3,2,1,0:T(8,128)S(1)}, f32[2,2,64,540]{3,2,1,0:T(8,128)}, u32[]{:S(2)}) copy-start(f32[2,2,64,540]{3,2,1,0:T(8,128)} %param.9) | copy-start | bytes 1658884
  322.2 75.3 %copy-start.4 = (f32[2,2,64,540]{3,2,1,0:T(8,128)}, f32[2,2,64,540]{3,2,1,0:T(8,128)S(1)}, u32[]{:S(2)}) copy-start(f32[2,2,64,540]{3,2,1,0:T(8,128)S(1)} %get-tuple-element.8) | copy-start | bytes 1658884
Sparse Core Ops, SparseCore 0:
  181.8 60.2 all-reduce.2
